TPU v7x, 512 devices: a whole 4x4x16 slice. The times are simulated.
512 devices in a mesh: seq: 64 (over z, y), head: 8 (over x, core).
Axes of the slice: x: 4, y: 4, z: 16, core: 2. Of those that a mesh axis runs over, the one named last changes fastest.
Arguments:
- queries: bfloat16 [32768, 4096], P(('seq', 'head')), may hold values from -8 to 8
- keys: bfloat16 [32768, 4096], P(('seq', 'head')), may hold values from -9 to 9
- values: bfloat16 [32768, 4096], P(('seq', 'head')), may hold values from -6 to 6
- grad_out: bfloat16 [32768, 4096], P(('seq', 'head')), may hold values from -6 to 6
- cluster_ids: int32 [32, 32768, 1], P('head', 'seq'), may hold values from 0 to 511; in each aligned block of 512 rows (0 to 511, 512 to 1023, ..., all dimensions but the last counted through in order) at most 2 rows name the same one
Outputs:
- attn_out: bfloat16 [32768, 4096], P(('seq', 'head'))
- query_gradient: bfloat16 [32768, 4096], P(('seq', 'head'))
- key_gradient: bfloat16 [32768, 4096], P(('seq', 'head'))
- value_gradient: bfloat16 [32768, 4096], P(('seq', 'head'))
Inputs may be any that keep to these rules, and one draw needn't show every extreme that they name: `cluster_ids`: in each head, among the 512 tokens of one index of seq, no cluster is named more than 2 times, and in every draw some cluster is named exactly 2 times there.
All inputs are finite; a program needn't handle non-finite values.
Results may differ from a plain program's by a relative error of at most 0.015.
Values may be sent and summed in bfloat16 or wider, within the bound.
A program may use at most 64 MiB of HBM per device.

v0:
```python
import jax
import jax.numpy as jnp
from jax import lax
from jax.sharding import PartitionSpec as P

HEAD_WIDTH = 128
CLUSTERS = 512
MOST = 2


def group_size(count, slots):
    group = 1
    while group * 2 <= count and count % (group * 2) == 0 and (group * 2 * slots <= 512):
        group = group * 2
    return group


def run_items(func, arrays):
    count = arrays[0].shape[0]
    heads_here = arrays[0].shape[1]
    group = group_size(count, arrays[0].shape[2])
    grouped = tuple((a.reshape((count // group, group * heads_here) + a.shape[2:]) for a in arrays))
    result = lax.map(func, grouped)
    return jax.tree.map(lambda r: r.reshape((count, heads_here) + r.shape[2:]), result)


def probabilities(query_block, key_block, valid):
    logit_scores = jnp.einsum(
        "rnl,rvl->rnv", query_block, key_block, preferred_element_type=jnp.float32
    ) * HEAD_WIDTH ** (-0.5)
    logit_scores = jnp.where(valid[:, None, :] > 0, logit_scores, -1e30)
    top = jnp.max(logit_scores, axis=2, keepdims=True)
    expo = jnp.exp(logit_scores - top)
    probs = expo / jnp.sum(expo, axis=2, keepdims=True)
    return (probs, probs.astype(jnp.bfloat16))


def combine(probability_block, value_block):
    return jnp.einsum(
        "xyl,xla->xya", probability_block, value_block, preferred_element_type=jnp.float32
    ).astype(jnp.bfloat16)


def gradients(probs, probability_block, query_block, key_block, value_block, output_gradient_block):
    probability_gradient = jnp.einsum(
        "rnl,rvl->rnv", output_gradient_block, value_block, preferred_element_type=jnp.float32
    )
    score_gradient = (
        probs
        * (probability_gradient - jnp.sum(probs * probability_gradient, axis=2, keepdims=True))
        * HEAD_WIDTH ** (-0.5)
    )
    score_gradient = score_gradient.astype(jnp.bfloat16)
    query_gradient = jnp.einsum(
        "xyl,xla->xya", score_gradient, key_block, preferred_element_type=jnp.float32
    ).astype(jnp.bfloat16)
    key_gradient = jnp.einsum(
        "hmf,hmw->hfw", score_gradient, query_block, preferred_element_type=jnp.float32
    ).astype(jnp.bfloat16)
    value_gradient = jnp.einsum(
        "hmf,hmw->hfw", probability_block, output_gradient_block, preferred_element_type=jnp.float32
    ).astype(jnp.bfloat16)
    return (query_gradient, key_gradient, value_gradient)


def forward_item(pieces):
    query_block, key_block, value_block, valid = pieces
    probs, probability_block = probabilities(query_block, key_block, valid)
    return combine(probability_block, value_block)


def backward_item(pieces):
    query_block, key_block, value_block, valid, output_gradient_block = pieces
    probs, probability_block = probabilities(query_block, key_block, valid)
    return gradients(
        probs, probability_block, query_block, key_block, value_block, output_gradient_block
    )


def body(queries, keys, values, grad_out, cluster_ids):
    q_rows, k_rows, v_rows, g_rows = (
        lax.all_to_all(queries, "head", split_axis=1, concat_axis=0, tiled=True),
        lax.all_to_all(keys, "head", split_axis=1, concat_axis=0, tiled=True),
        lax.all_to_all(values, "head", split_axis=1, concat_axis=0, tiled=True),
        lax.all_to_all(grad_out, "head", split_axis=1, concat_axis=0, tiled=True),
    )
    tok_rows = q_rows.shape[0]
    heads_here = cluster_ids.shape[0]
    seq_count = lax.axis_size("seq")
    per_owner = CLUSTERS // seq_count
    slots = seq_count * MOST
    total = per_owner * heads_here * slots
    ids = cluster_ids[:, :, 0]
    onehot = (ids[:, :, None] == jnp.arange(CLUSTERS, dtype=jnp.int32)[None, None, :]).astype(
        jnp.bfloat16
    )
    row_pos = lax.broadcasted_iota(jnp.int32, (tok_rows, tok_rows), 0)
    col_pos = lax.broadcasted_iota(jnp.int32, (tok_rows, tok_rows), 1)
    lower = (row_pos >= col_pos).astype(jnp.bfloat16)
    running = jnp.einsum("st,htc->hsc", lower, onehot, preferred_element_type=jnp.float32)
    rank = (jnp.sum(running * onehot, axis=2) - 1.0).astype(jnp.int32)
    owner = ids % seq_count
    local = ids // seq_count
    head_pos = lax.broadcasted_iota(jnp.int32, ids.shape, 0)
    target = ((local * heads_here + head_pos) * slots + owner * MOST + rank).T.reshape(-1)

    def pack(rows):
        flat = (
            jnp.zeros((total, HEAD_WIDTH), rows.dtype).at[target].set(rows.reshape(-1, HEAD_WIDTH))
        )
        return flat.reshape(per_owner, heads_here, slots, HEAD_WIDTH)

    def unpack(buffer):
        return buffer.reshape(total, HEAD_WIDTH)[target].reshape(tok_rows, heads_here * HEAD_WIDTH)

    valid = (
        jnp.zeros((total,), jnp.bfloat16).at[target].set(1).reshape(per_owner, heads_here, slots)
    )
    q_buf = pack(q_rows)
    k_buf = pack(k_rows)
    v_buf = pack(v_rows)
    g_buf = pack(g_rows)
    q_in, k_in, v_in, valid_in = (
        lax.all_to_all(q_buf, "seq", split_axis=2, concat_axis=2, tiled=True),
        lax.all_to_all(k_buf, "seq", split_axis=2, concat_axis=2, tiled=True),
        lax.all_to_all(v_buf, "seq", split_axis=2, concat_axis=2, tiled=True),
        lax.all_to_all(valid, "seq", split_axis=2, concat_axis=2, tiled=True),
    )
    out_own = run_items(forward_item, (q_in, k_in, v_in, valid_in))
    out_back = lax.all_to_all(out_own, "seq", split_axis=2, concat_axis=2, tiled=True)
    g_in = lax.all_to_all(g_buf, "seq", split_axis=2, concat_axis=2, tiled=True)
    dq_own, dk_own, dv_own = run_items(backward_item, (q_in, k_in, v_in, valid_in, g_in))
    dq_back, dk_back, dv_back = (
        lax.all_to_all(dq_own, "seq", split_axis=2, concat_axis=2, tiled=True),
        lax.all_to_all(dk_own, "seq", split_axis=2, concat_axis=2, tiled=True),
        lax.all_to_all(dv_own, "seq", split_axis=2, concat_axis=2, tiled=True),
    )
    return (
        lax.all_to_all(unpack(out_back), "head", split_axis=0, concat_axis=1, tiled=True),
        lax.all_to_all(unpack(dq_back), "head", split_axis=0, concat_axis=1, tiled=True),
        lax.all_to_all(unpack(dk_back), "head", split_axis=0, concat_axis=1, tiled=True),
        lax.all_to_all(unpack(dv_back), "head", split_axis=0, concat_axis=1, tiled=True),
    )


def solution(mesh):
    return jax.shard_map(
        body,
        mesh=mesh,
        in_specs=(
            P(("seq", "head"), None),
            P(("seq", "head"), None),
            P(("seq", "head"), None),
            P(("seq", "head"), None),
            P("head", "seq", None),
        ),
        out_specs=(
            P(("seq", "head"), None),
            P(("seq", "head"), None),
            P(("seq", "head"), None),
            P(("seq", "head"), None),
        ),
        check_vma=False,
    )
```

profile of v0, /device:TPU:1, one launch (start us, length us, event | category | flops | bytes accessed | tf_op | source)
XLA Modules:
  0.0 650.6 jit_solution(9257804042346916714)
XLA Ops:
  1.3 1.7 fusion.79
  3.5 14.6 %scatter_custom_fusion = bf16[4096]{0:T(1024)(128)(2,1)S(1)} fusion(s32[2048]{0:T(1024)S(1)} %bitcast.193, bf16[2048]{0:T(1024)(128)(2,1)S(1)} %broadcast.77, bf16[]{:T(256)} %constant.82.clone.1), kind=kCustom, calls=%fused_computation.121 | custom fusion | bytes 8194 | tf_op jit(solution)/shard_map/scatter | solution.py:117
  18.9 19.3 %all-to-all-start = ((bf16[8,4,128]{0,1,2:T(4,128)(2,1)}), bf16[8,4,128]{0,1,2:T(4,128)(2,1)S(1)}, u32[]{:S(2)}, u32[]{:S(2)}) async-start(bf16[8,4,128]{0,1,2:T(4,128)(2,1)} %copy.89), calls=%async_computation | async-start | bytes 262144 | tf_op jit(solution)/shard_map/all_to_all | solution.py:127
  39.1 14.2 %all-to-all-done = bf16[8,4,128]{0,1,2:T(4,128)(2,1)S(1)} async-done(((bf16[8,4,128]{0,1,2:T(4,128)(2,1)}), bf16[8,4,128]{0,1,2:T(4,128)(2,1)S(1)}, u32[]{:S(2)}, u32[]{:S(2)}) %all-to-all-start) | async-done | bytes 8224 | tf_op jit(solution)/shard_map/all_to_all | solution.py:127
  53.3 7.9 %all-to-all-start.1 = ((bf16[64,8,512]{2,0,1:T(8,128)(2,1)}), bf16[64,8,512]{2,0,1:T(8,128)(2,1)S(1)}, u32[]{:S(2)}, u32[]{:S(2)}) async-start(bf16[64,8,512]{2,0,1:T(8,128)(2,1)} %bitcast.125), calls=%async_computation.1 | async-start | bytes 1048576 | tf_op jit(solution)/shard_map/all_to_all | solution.py:82
  62.0 8.5 %all-to-all-done.1 = bf16[64,8,512]{2,0,1:T(8,128)(2,1)S(1)} async-done(((bf16[64,8,512]{2,0,1:T(8,128)(2,1)}), bf16[64,8,512]{2,0,1:T(8,128)(2,1)S(1)}, u32[]{:S(2)}, u32[]{:S(2)}) %all-to-all-start.1) | async-done | bytes 524320 | tf_op jit(solution)/shard_map/all_to_all | solution.py:82
  70.5 4.4 all-to-all-start.3
  75.7 8.5 %all-to-all-done.3 = bf16[64,8,512]{2,0,1:T(8,128)(2,1)S(1)} async-done(((bf16[64,8,512]{2,0,1:T(8,128)(2,1)}), bf16[64,8,512]{2,0,1:T(8,128)(2,1)S(1)}, u32[]{:S(2)}, u32[]{:S(2)}) %all-to-all-start.3) | async-done | bytes 524320 | tf_op jit(solution)/shard_map/all_to_all | solution.py:83
  84.2 4.4 all-to-all-start.5
  89.4 8.5 %all-to-all-done.5 = bf16[64,8,512]{2,0,1:T(8,128)(2,1)S(1)} async-done(((bf16[64,8,512]{2,0,1:T(8,128)(2,1)}), bf16[64,8,512]{2,0,1:T(8,128)(2,1)S(1)}, u32[]{:S(2)}, u32[]{:S(2)}) %all-to-all-start.5) | async-done | bytes 524320 | tf_op jit(solution)/shard_map/all_to_all | solution.py:84
  98.0 4.4 all-to-all-start.9
  103.4 6.4 scatter_custom_fusion.1
  109.9 1.8 copy.92
  112.5 4.8 all-to-all-start.2
  118.5 6.4 scatter_custom_fusion.2
  124.9 1.8 copy.94
  126.7 42.8 %all-to-all-done.2 = bf16[8,4,128,128]{3,1,0,2:T(4,128)(2,1)S(1)} async-done(((bf16[8,4,128,128]{3,1,0,2:T(4,128)(2,1)}), bf16[8,4,128,128]{3,1,0,2:T(4,128)(2,1)S(1)}, u32[]{:S(2)}, u32[]{:S(2)}) %all-to-all-start.2) | async-done | bytes 1048608 | tf_op jit(solution)/shard_map/all_to_all | solution.py:124
  169.5 8.1 %all-to-all-start.4 = ((bf16[8,4,128,128]{3,1,0,2:T(4,128)(2,1)}), bf16[8,4,128,128]{3,1,0,2:T(4,128)(2,1)S(1)}, u32[]{:S(2)}, u32[]{:S(2)}) async-start(bf16[8,4,128,128]{3,1,0,2:T(4,128)(2,1)} %copy.94), calls=%async_computation.4 | async-start | bytes 2097152 | tf_op jit(solution)/shard_map/all_to_all | solution.py:125
  178.7 6.4 scatter_custom_fusion.3
  185.1 1.8 copy.96
  186.9 42.2 %all-to-all-done.4 = bf16[8,4,128,128]{3,1,0,2:T(4,128)(2,1)S(1)} async-done(((bf16[8,4,128,128]{3,1,0,2:T(4,128)(2,1)}), bf16[8,4,128,128]{3,1,0,2:T(4,128)(2,1)S(1)}, u32[]{:S(2)}, u32[]{:S(2)}) %all-to-all-start.4) | async-done | bytes 1048608 | tf_op jit(solution)/shard_map/all_to_all | solution.py:125
  230.1 8.4 %all-to-all-start.6 = ((bf16[8,4,128,128]{3,1,0,2:T(4,128)(2,1)}), bf16[8,4,128,128]{3,1,0,2:T(4,128)(2,1)}, u32[]{:S(2)}, u32[]{:S(2)}) async-start(bf16[8,4,128,128]{3,1,0,2:T(4,128)(2,1)} %copy.96), calls=%async_computation.6 | async-start | bytes 2097152 | tf_op jit(solution)/shard_map/all_to_all | solution.py:126
  238.9 6.1 scatter_custom_fusion.4
  244.9 1.8 copy.104
  246.7 42.2 %all-to-all-done.6 = bf16[8,4,128,128]{3,1,0,2:T(4,128)(2,1)} async-done(((bf16[8,4,128,128]{3,1,0,2:T(4,128)(2,1)}), bf16[8,4,128,128]{3,1,0,2:T(4,128)(2,1)}, u32[]{:S(2)}, u32[]{:S(2)}) %all-to-all-start.6) | async-done | bytes 1048608 | tf_op jit(solution)/shard_map/all_to_all | solution.py:126
  288.9 8.8 %all-to-all-start.10 = ((bf16[8,4,128,128]{3,1,0,2:T(4,128)(2,1)}), bf16[8,4,128,128]{3,1,0,2:T(4,128)(2,1)S(1)}, u32[]{:S(2)}, u32[]{:S(2)}) async-start(bf16[8,4,128,128]{3,1,0,2:T(4,128)(2,1)} %copy.104), calls=%async_computation.10 | async-start | bytes 2097152 | tf_op jit(solution)/shard_map/all_to_all | solution.py:131
  300.5 2.6 copy.99
  304.3 8.8 %while.24 = (s32[]{:T(128)}, bf16[2,16,128,128]{3,1,0,2:T(8,128)(2,1)}, bf16[2,16,128]{2,1,0:T(8,128)(2,1)S(1)}, bf16[2,16,128,128]{3,2,1,0:T(8,128)(2,1)S(1)}, ...) while((s32[]{:T(128)}, bf16[2,16,128,128]{3,1,0,2:T(8,128)(2,1)}, ...), condition=%wide.region_8.9_spmd, body=%wide.region_5.8_spmd.sunk | while | flops 136054912 | bytes 5268577 | solution.py:23
  304.3 1.8 fusion.135
  308.7 1.8 fusion.135
  313.1 34.1 %all-to-all-done.10 = bf16[8,4,128,128]{3,1,0,2:T(4,128)(2,1)S(1)} async-done(((bf16[8,4,128,128]{3,1,0,2:T(4,128)(2,1)}), bf16[8,4,128,128]{3,1,0,2:T(4,128)(2,1)S(1)}, u32[]{:S(2)}, u32[]{:S(2)}) %all-to-all-start.10) | async-done | bytes 1048608 | tf_op jit(solution)/shard_map/all_to_all | solution.py:131
  347.2 10.1 %all-to-all-start.7 = ((bf16[8,4,128,128]{3,1,0,2:T(4,128)(2,1)}), bf16[8,4,128,128]{3,1,0,2:T(4,128)(2,1)}, u32[]{:S(2)}, u32[]{:S(2)}) async-start(bf16[8,4,128,128]{3,1,0,2:T(4,128)(2,1)} %bitcast.28), calls=%async_computation.7 | async-start | bytes 2097152 | tf_op jit(solution)/shard_map/all_to_all | solution.py:130
  360.7 29.9 %while.25 = (s32[]{:T(128)}, bf16[2,16,128,128]{3,1,0,2:T(8,128)(2,1)}, bf16[2,16,128,128]{3,1,0,2:T(8,128)(2,1)}, bf16[2,16,128,128]{3,1,0,2:T(8,128)(2,1)}, bf...) while((s32[]{:T(128)}, ...), condition=%wide.region_14.15_spmd, body=%wide.region_10.14_spmd.sunk | while | flops 341580160 | bytes 46196016 | solution.py:23
  361.7 1.5 fusion.145
  363.2 2.6 fusion.146
  367.4 2.1 fusion.149
  369.5 2.2 fusion.147
  372.9 1.6 copy_dynamic-update-slice_fusion.9
  378.1 2.6 fusion.146
  382.3 2.1 fusion.149
  384.4 2.3 fusion.147
  387.9 1.6 copy_dynamic-update-slice_fusion.9
  390.5 15.9 %all-to-all-done.7 = bf16[8,4,128,128]{3,1,0,2:T(4,128)(2,1)} async-done(((bf16[8,4,128,128]{3,1,0,2:T(4,128)(2,1)}), bf16[8,4,128,128]{3,1,0,2:T(4,128)(2,1)}, u32[]{:S(2)}, u32[]{:S(2)}) %all-to-all-start.7) | async-done | bytes 1048608 | tf_op jit(solution)/shard_map/all_to_all | solution.py:130
  406.4 59.2 %all_to_all.185 = bf16[8,4,128,128]{3,1,0,2:T(4,128)(2,1)} all-to-all(bf16[8,4,128,128]{3,1,0,2:T(4,128)(2,1)} %bitcast.171), channel_id=1, replica_groups=mesh['seq'=64,'head'=8] {'seq'}, dimensions={2} | all-to-all | bytes 2097152 | tf_op jit(solution)/shard_map/all_to_all | solution.py:134
  465.6 58.8 %all_to_all.186 = bf16[8,4,128,128]{3,1,0,2:T(4,128)(2,1)S(1)} all-to-all(bf16[8,4,128,128]{3,1,0,2:T(4,128)(2,1)S(1)} %bitcast.172), channel_id=1, replica_groups=mesh['seq'=64,'head'=8] {'seq'}, dimensions={2} | all-to-all | bytes 2097152 | tf_op jit(solution)/shard_map/all_to_all | solution.py:136
  524.4 9.6 %all-to-all-start.13 = ((bf16[8,4,128,128]{3,1,0,2:T(4,128)(2,1)}), bf16[8,4,128,128]{3,1,0,2:T(4,128)(2,1)S(1)}, u32[]{:S(2)}, u32[]{:S(2)}) async-start(bf16[8,4,128,128]{3,1,0,2:T(4,128)(2,1)} %bitcast.37), calls=%async_computation.13 | async-start | bytes 2097152 | tf_op jit(solution)/shard_map/all_to_all | solution.py:135
  534.0 1.6 copy.101
  535.7 8.1 %gather_fusion = bf16[2048,128]{1,0:T(8,128)(2,1)} fusion(bf16[4096,128]{1,0:T(8,128)(2,1)S(1)} %bitcast.165, s32[2048]{0:T(1024)S(1)} %broadcast_clamp_fusion), kind=kCustom, calls=%fused_computation | custom fusion | bytes 1056768 | tf_op jit(solution)/shard_map/gather | solution.py:114
  543.7 2.1 all_to_all.145
  545.9 37.5 %all-to-all-done.13 = bf16[8,4,128,128]{3,1,0,2:T(4,128)(2,1)S(1)} async-done(((bf16[8,4,128,128]{3,1,0,2:T(4,128)(2,1)}), bf16[8,4,128,128]{3,1,0,2:T(4,128)(2,1)S(1)}, u32[]{:S(2)}, u32[]{:S(2)}) %all-to-all-start.13) | async-done | bytes 1048608 | tf_op jit(solution)/shard_map/all_to_all | solution.py:135
  583.3 12.4 %all-to-all-start.8 = ((bf16[8,64,512]{2,1,0:T(8,128)(2,1)}), bf16[8,64,512]{2,1,0:T(8,128)(2,1)}, u32[]{:S(2)}, u32[]{:S(2)}) async-start(bf16[8,64,512]{2,1,0:T(8,128)(2,1)} %all_to_all.145), calls=%async_computation.8 | async-start | bytes 1048576 | tf_op jit(solution)/shard_map/all_to_all | solution.py:139
  595.8 1.6 copy.110
  597.4 8.1 %gather_fusion.1 = bf16[2048,128]{1,0:T(8,128)(2,1)} fusion(bf16[4096,128]{1,0:T(8,128)(2,1)S(1)} %bitcast.166, s32[2048]{0:T(1024)S(1)} %broadcast_clamp_fusion), kind=kCustom, calls=%fused_computation.1 | custom fusion | bytes 1056768 | tf_op jit(solution)/shard_map/gather | solution.py:114
  605.4 2.1 all_to_all.154
  607.6 4.8 all-to-all-start.12
  612.8 6.2 gather_fusion.3
  620.1 1.7 all-to-all-done.12
  621.8 4.4 all-to-all-start.16
  626.6 6.2 gather_fusion.2
  633.9 1.7 all-to-all-done.16
  635.6 4.4 all-to-all-start.14
  640.0 1.9 copy.134
  641.8 1.9 copy.135
  644.6 4.8 all-to-all-done.14
  (90 shorter events, 39.2 us)
Async XLA Ops:
  1.3 1.8 copy-start.15
  3.1 35.1 %copy-start.11 = (bf16[64,4096]{1,0:T(8,128)(2,1)S(1)}, bf16[64,4096]{1,0:T(8,128)(2,1)}, u32[]{:S(2)}) copy-start(bf16[64,4096]{1,0:T(8,128)(2,1)} %param.9) | copy-start | bytes 1572868
  18.9 34.3 %all-to-all-start = ((bf16[8,4,128]{0,1,2:T(4,128)(2,1)}), bf16[8,4,128]{0,1,2:T(4,128)(2,1)S(1)}, u32[]{:S(2)}, u32[]{:S(2)}) async-start(bf16[8,4,128]{0,1,2:T(4,128)(2,1)} %copy.89), calls=%async_computation | async-start | bytes 262144 | tf_op jit(solution)/shard_map/all_to_all | solution.py:127
  38.2 22.9 %copy-start.12 = (bf16[64,4096]{1,0:T(8,128)(2,1)S(1)}, bf16[64,4096]{1,0:T(8,128)(2,1)}, u32[]{:S(2)}) copy-start(bf16[64,4096]{1,0:T(8,128)(2,1)} %param.10) | copy-start | bytes 1572868
  53.3 17.2 %all-to-all-start.1 = ((bf16[64,8,512]{2,0,1:T(8,128)(2,1)}), bf16[64,8,512]{2,0,1:T(8,128)(2,1)S(1)}, u32[]{:S(2)}, u32[]{:S(2)}) async-start(bf16[64,8,512]{2,0,1:T(8,128)(2,1)} %bitcast.125), calls=%async_computation.1 | async-start | bytes 1048576 | tf_op jit(solution)/shard_map/all_to_all | solution.py:82
  61.1 13.7 %copy-start.13 = (bf16[64,4096]{1,0:T(8,128)(2,1)S(1)}, bf16[64,4096]{1,0:T(8,128)(2,1)}, u32[]{:S(2)}) copy-start(bf16[64,4096]{1,0:T(8,128)(2,1)} %param.11) | copy-start | bytes 1572868
  70.5 13.7 %all-to-all-start.3 = ((bf16[64,8,512]{2,0,1:T(8,128)(2,1)}), bf16[64,8,512]{2,0,1:T(8,128)(2,1)S(1)}, u32[]{:S(2)}, u32[]{:S(2)}) async-start(bf16[64,8,512]{2,0,1:T(8,128)(2,1)} %bitcast.124), calls=%async_computation.3 | async-start | bytes 1048576 | tf_op jit(solution)/shard_map/all_to_all | solution.py:83
  74.9 13.7 %copy-start.14 = (bf16[64,4096]{1,0:T(8,128)(2,1)S(1)}, bf16[64,4096]{1,0:T(8,128)(2,1)}, u32[]{:S(2)}) copy-start(bf16[64,4096]{1,0:T(8,128)(2,1)} %param.12) | copy-start | bytes 1572868
  84.2 13.7 %all-to-all-start.5 = ((bf16[64,8,512]{2,0,1:T(8,128)(2,1)}), bf16[64,8,512]{2,0,1:T(8,128)(2,1)S(1)}, u32[]{:S(2)}, u32[]{:S(2)}) async-start(bf16[64,8,512]{2,0,1:T(8,128)(2,1)} %bitcast.123), calls=%async_computation.5 | async-start | bytes 1048576 | tf_op jit(solution)/shard_map/all_to_all | solution.py:84
  98.0 13.7 %all-to-all-start.9 = ((bf16[64,8,512]{2,0,1:T(8,128)(2,1)}), bf16[64,8,512]{2,0,1:T(8,128)(2,1)S(1)}, u32[]{:S(2)}, u32[]{:S(2)}) async-start(bf16[64,8,512]{2,0,1:T(8,128)(2,1)} %bitcast.122), calls=%async_computation.9 | async-start | bytes 1048576 | tf_op jit(solution)/shard_map/all_to_all | solution.py:85
  111.7 0.8 copy-start.7
  112.5 57.0 %all-to-all-start.2 = ((bf16[8,4,128,128]{3,1,0,2:T(4,128)(2,1)}), bf16[8,4,128,128]{3,1,0,2:T(4,128)(2,1)S(1)}, u32[]{:S(2)}, u32[]{:S(2)}) async-start(bf16[8,4,128,128]{3,1,0,2:T(4,128)(2,1)} %copy.92), calls=%async_computation.2 | async-start | bytes 2097152 | tf_op jit(solution)/shard_map/all_to_all | solution.py:124
  169.5 59.6 %all-to-all-start.4 = ((bf16[8,4,128,128]{3,1,0,2:T(4,128)(2,1)}), bf16[8,4,128,128]{3,1,0,2:T(4,128)(2,1)S(1)}, u32[]{:S(2)}, u32[]{:S(2)}) async-start(bf16[8,4,128,128]{3,1,0,2:T(4,128)(2,1)} %copy.94), calls=%async_computation.4 | async-start | bytes 2097152 | tf_op jit(solution)/shard_map/all_to_all | solution.py:125
  186.9 51.6 %copy-start.8 = (bf16[64,8,512]{2,0,1:T(8,128)(2,1)S(1)}, bf16[64,8,512]{2,0,1:T(8,128)(2,1)}, u32[]{:S(2)}) copy-start(bf16[64,8,512]{2,0,1:T(8,128)(2,1)} %copy-done.7) | copy-start | bytes 1572868
  229.1 1.0 copy-start.2
  230.1 58.8 %all-to-all-start.6 = ((bf16[8,4,128,128]{3,1,0,2:T(4,128)(2,1)}), bf16[8,4,128,128]{3,1,0,2:T(4,128)(2,1)}, u32[]{:S(2)}, u32[]{:S(2)}) async-start(bf16[8,4,128,128]{3,1,0,2:T(4,128)(2,1)} %copy.96), calls=%async_computation.6 | async-start | bytes 2097152 | tf_op jit(solution)/shard_map/all_to_all | solution.py:126
  288.9 58.3 %all-to-all-start.10 = ((bf16[8,4,128,128]{3,1,0,2:T(4,128)(2,1)}), bf16[8,4,128,128]{3,1,0,2:T(4,128)(2,1)S(1)}, u32[]{:S(2)}, u32[]{:S(2)}) async-start(bf16[8,4,128,128]{3,1,0,2:T(4,128)(2,1)} %copy.104), calls=%async_computation.10 | async-start | bytes 2097152 | tf_op jit(solution)/shard_map/all_to_all | solution.py:131
  297.8 1.2 copy-start.3
  347.2 59.2 %all-to-all-start.7 = ((bf16[8,4,128,128]{3,1,0,2:T(4,128)(2,1)}), bf16[8,4,128,128]{3,1,0,2:T(4,128)(2,1)}, u32[]{:S(2)}, u32[]{:S(2)}) async-start(bf16[8,4,128,128]{3,1,0,2:T(4,128)(2,1)} %bitcast.28), calls=%async_computation.7 | async-start | bytes 2097152 | tf_op jit(solution)/shard_map/all_to_all | solution.py:130
  360.7 1.0 copy-start
  360.7 6.7 %copy-start.9 = (bf16[2,16,128,128]{3,2,1,0:T(8,128)(2,1)}, bf16[2,16,128,128]{3,2,1,0:T(8,128)(2,1)S(1)}, u32[]{:S(2)}) copy-start(bf16[2,16,128,128]{3,2,1,0:T(8,128)(2,1)S(1)} %get-tuple-element.320) | copy-start | bytes 3145732 | tf_op jit(solution)/shard_map/while
  371.7 1.2 copy-start.4
  372.9 2.7 copy-start.1
  372.9 2.7 copy-start.10
  374.6 1.0 copy-start.5
  375.6 1.0 copy-start
  375.6 6.7 %copy-start.9 = (bf16[2,16,128,128]{3,2,1,0:T(8,128)(2,1)}, bf16[2,16,128,128]{3,2,1,0:T(8,128)(2,1)S(1)}, u32[]{:S(2)}) copy-start(bf16[2,16,128,128]{3,2,1,0:T(8,128)(2,1)S(1)} %get-tuple-element.320) | copy-start | bytes 3145732 | tf_op jit(solution)/shard_map/while
  386.7 1.2 copy-start.4
  387.9 2.6 copy-start.1
  387.9 2.6 copy-start.10
  389.5 1.0 copy-start.5
  406.4 59.2 %copy-start.6 = (bf16[2,16,128,128]{3,1,0,2:T(8,128)(2,1)S(1)}, bf16[2,16,128,128]{3,1,0,2:T(8,128)(2,1)}, u32[]{:S(2)}) copy-start(bf16[2,16,128,128]{3,1,0,2:T(8,128)(2,1)} %get-tuple-element.88) | copy-start | bytes 3145732
  524.4 58.9 %all-to-all-start.13 = ((bf16[8,4,128,128]{3,1,0,2:T(4,128)(2,1)}), bf16[8,4,128,128]{3,1,0,2:T(4,128)(2,1)S(1)}, u32[]{:S(2)}, u32[]{:S(2)}) async-start(bf16[8,4,128,128]{3,1,0,2:T(4,128)(2,1)} %bitcast.37), calls=%async_computation.13 | async-start | bytes 2097152 | tf_op jit(solution)/shard_map/all_to_all | solution.py:135
  583.3 24.3 %all-to-all-start.8 = ((bf16[8,64,512]{2,1,0:T(8,128)(2,1)}), bf16[8,64,512]{2,1,0:T(8,128)(2,1)}, u32[]{:S(2)}, u32[]{:S(2)}) async-start(bf16[8,64,512]{2,1,0:T(8,128)(2,1)} %all_to_all.145), calls=%async_computation.8 | async-start | bytes 1048576 | tf_op jit(solution)/shard_map/all_to_all | solution.py:139
  607.6 14.3 %all-to-all-start.12 = ((bf16[8,64,512]{2,1,0:T(8,128)(2,1)}), bf16[8,64,512]{2,1,0:T(8,128)(2,1)}, u32[]{:S(2)}, u32[]{:S(2)}) async-start(bf16[8,64,512]{2,1,0:T(8,128)(2,1)} %all_to_all.154), calls=%async_computation.12 | async-start | bytes 1048576 | tf_op jit(solution)/shard_map/all_to_all | solution.py:140
  621.8 13.7 %all-to-all-start.16 = ((bf16[8,64,512]{2,1,0:T(8,128)(2,1)}), bf16[8,64,512]{2,1,0:T(8,128)(2,1)S(1)}, u32[]{:S(2)}, u32[]{:S(2)}) async-start(bf16[8,64,512]{2,1,0:T(8,128)(2,1)} %all_to_all.164), calls=%async_computation.16 | async-start | bytes 1048576 | tf_op jit(solution)/shard_map/all_to_all | solution.py:142
  635.6 13.7 %all-to-all-start.14 = ((bf16[8,64,512]{2,1,0:T(8,128)(2,1)}), bf16[8,64,512]{2,1,0:T(8,128)(2,1)S(1)}, u32[]{:S(2)}, u32[]{:S(2)}) async-start(bf16[8,64,512]{2,1,0:T(8,128)(2,1)} %all_to_all.159), calls=%async_computation.14 | async-start | bytes 1048576 | tf_op jit(solution)/shard_map/all_to_all | solution.py:141
where the time goes:
time: 661 us; the launch traced here: 651 us
  waiting for transfers between devices  263 us (40%)
  local copies, waits for them, and re-layouts  124 us (19%)
  blocking collectives  118 us (18%)
  starting transfers between devices  116 us (18%)
  matrix products  28 us (4%)
    all_to_all x1, blocking collectives, body(): lax.all_to_all(dq_own, 'seq', split_axis=2, concat_axis=2, tiled=True)  59.2 us
    all_to_all x1, blocking collectives, body(): lax.all_to_all(dv_own, 'seq', split_axis=2, concat_axis=2, tiled=True)  58.8 us
    all_to_all x1, waiting for transfers between devices, body(): lax.all_to_all(q_buf, 'seq', split_axis=2, concat_axis=2, tiled=True)  42.8 us
    all_to_all x1, waiting for transfers between devices, body(): lax.all_to_all(k_buf, 'seq', split_axis=2, concat_axis=2, tiled=True)  42.2 us
    all_to_all x1, waiting for transfers between devices, body(): lax.all_to_all(v_buf, 'seq', split_axis=2, concat_axis=2, tiled=True)  42.2 us
    all_to_all x1, waiting for transfers between devices, body(): lax.all_to_all(dk_own, 'seq', split_axis=2, concat_axis=2, tiled=True)  37.5 us
    all_to_all x1, waiting for transfers between devices, body(): g_in = lax.all_to_all(g_buf, 'seq', split_axis=2, concat_axis=2, tiled=True)  34.1 us
    gather x4, local copies, waits for them, and re-layouts, unpack(): buffer.reshape(total, HEAD_WIDTH)[target]  28.5 us
  transfers between devices with their start and end apart: 15, of which 14 were waited for; matrix products, arithmetic and copies ran while one was open for 18% of the time, Pallas kernels for 0%

commit v1 on v0

v1 whole, which is shorter than its diff:
```python
import functools

import jax
import jax.numpy as jnp
from jax import lax
from jax.experimental import pallas as pl
from jax.experimental.pallas import tpu as pltpu
from jax.sharding import PartitionSpec as P

WIDTH = 128
CLUSTERS = 512
MOST = 2
TIGHT = 144
F32 = jnp.float32
BF16 = jnp.bfloat16
MESH = pl.DeviceIdType.MESH
BLOCK_Q = 256
NEG = -1e30


def iota(shape, dim):
    return lax.broadcasted_iota(jnp.int32, shape, dim)


def dot_nt(a, b):
    return lax.dot_general(a, b, (((1,), (1,)), ((), ())), preferred_element_type=F32)


def dot_tn(a, b):
    return lax.dot_general(a, b, (((0,), (0,)), ((), ())), preferred_element_type=F32)


def dot(a, b):
    return jnp.dot(a, b, preferred_element_type=F32)


def kernel(
    dims,
    q_ref, k_ref, v_ref, g_ref, ids_ref,
    out_ref, flag_ref,
    ids_buf, cnt_send, cnt_buf, flag_buf, rank_buf, pos_buf,
    rows, zsend, zrecv, zret, prob, marks, dk_acc, dv_acc,
    ids_sem, cnt_sem, flag_sem, one_sem, in_sem, back_sem, two_sem, own_sem,
):
    planes, lanes_y, groups, cap, per_dev = dims
    slots = planes * cap
    peers = lanes_y * groups
    seq_tok = groups * per_dev
    tokens = lanes_y * seq_tok
    chunks = tokens // 128
    per_seq = seq_tok // 128
    seq = lax.axis_index("seq")
    hd = lax.axis_index("head")
    z = seq // lanes_y
    y = seq % lanes_y
    mine = y * groups + hd

    def plane_peer(j):
        other_y = lax.rem(y + j // groups, lanes_y)
        other_h = lax.rem(hd + lax.rem(j, groups), groups)
        return other_y, other_h

    def plane_id(other_y, other_h):
        return (z * lanes_y + other_y, other_h)

    def ring_id(other_z):
        return (other_z * lanes_y + y, hd)

    barrier = pltpu.get_barrier_semaphore()

    @pl.loop(1, peers)
    def _(j):
        pl.semaphore_signal(barrier, inc=1, device_id=plane_id(*plane_peer(j)), device_id_type=MESH)

    @pl.loop(1, planes)
    def _(d):
        pl.semaphore_signal(
            barrier, inc=1, device_id=ring_id(lax.rem(z + d, planes)), device_id_type=MESH
        )

    pl.semaphore_wait(barrier, peers - 1 + planes - 1)

    @pl.loop(1, lanes_y)
    def _(d):
        other = lax.rem(y + d, lanes_y)
        pltpu.make_async_remote_copy(
            src_ref=ids_ref.at[other], dst_ref=ids_buf.at[y],
            send_sem=ids_sem.at[0], recv_sem=ids_sem.at[1],
            device_id=plane_id(other, hd), device_id_type=MESH,
        ).start()

    own_ids = pltpu.make_async_copy(ids_ref.at[y], ids_buf.at[y], own_sem.at[4])
    own_ids.start()

    own_copies = []
    for ti, ref in enumerate((q_ref, k_ref, v_ref, g_ref)):

        @pl.loop(1, peers)
        def _(j, ti=ti, ref=ref):
            other_y, other_h = plane_peer(j)
            head = other_h * lanes_y + other_y
            pltpu.make_async_remote_copy(
                src_ref=ref.at[:, pl.ds(pl.multiple_of(head * WIDTH, WIDTH), WIDTH)],
                dst_ref=rows.at[ti, pl.ds(pl.multiple_of(mine * per_dev, per_dev), per_dev), :],
                send_sem=one_sem.at[0, ti], recv_sem=one_sem.at[1, ti],
                device_id=plane_id(other_y, other_h), device_id_type=MESH,
            ).start()

        head = hd * lanes_y + y
        copy = pltpu.make_async_copy(
            ref.at[:, pl.ds(pl.multiple_of(head * WIDTH, WIDTH), WIDTH)],
            rows.at[ti, pl.ds(pl.multiple_of(mine * per_dev, per_dev), per_dev), :],
            own_sem.at[ti],
        )
        copy.start()
        own_copies.append(copy)

    def drain(ref, sem):
        pltpu.make_async_copy(ref, ref, sem).wait()

    own_ids.wait()
    drain(ids_buf.at[pl.ds(0, lanes_y - 1)], ids_sem.at[1])

    tri = jnp.where(iota((128, 128), 0) <= iota((128, 128), 1), 1.0, 0.0).astype(BF16)
    full = jnp.ones((128, 128), BF16)
    tri_full = jnp.concatenate([tri, full], axis=1)
    eye = iota((128, 128), 0) == iota((128, 128), 1)

    def ids_row(ch):
        return ids_buf[ch // per_seq, pl.ds(lax.rem(ch, per_seq), 1), :]

    def rank_step(ch, carry):
        member = iota((CLUSTERS, 128), 0) == ids_row(ch)
        both = dot(jnp.where(member, 1.0, 0.0).astype(BF16), tri_full)
        rank = jnp.sum(
            jnp.where(member, both[:, :128] + carry - 1.0, 0.0), axis=0, keepdims=True
        )
        rank_buf[pl.ds(ch, 1), :] = rank
        return carry + both[:, 128:]

    sizes = lax.fori_loop(0, chunks, rank_step, jnp.zeros((CLUSTERS, 128), F32))

    def col_to_row(col):
        return jnp.concatenate(
            [
                jnp.sum(jnp.where(eye, col[i:i + 128, :], 0.0), axis=0, keepdims=True)
                for i in range(0, CLUSTERS, 128)
            ],
            axis=1,
        )

    def row_to_col(row):
        return jnp.concatenate(
            [
                jnp.sum(jnp.where(eye, row[:, i:i + 128], 0.0), axis=1, keepdims=True)
                for i in range(0, row.shape[1], 128)
            ],
            axis=0,
        )

    size_row = col_to_row(sizes)
    cnt_send[...] = size_row
    cnt_buf[z] = size_row

    @pl.loop(1, planes)
    def _(d):
        pltpu.make_async_remote_copy(
            src_ref=cnt_send, dst_ref=cnt_buf.at[z],
            send_sem=cnt_sem.at[0], recv_sem=cnt_sem.at[1],
            device_id=ring_id(lax.rem(z + d, planes)), device_id_type=MESH,
        ).start()

    drain(cnt_buf.at[pl.ds(0, planes - 1)], cnt_sem.at[1])
    drain(cnt_buf.at[pl.ds(0, planes - 1)], cnt_sem.at[0])

    counts = jnp.concatenate([cnt_buf[i] for i in range(planes)], axis=0)
    total = jnp.sum(counts, axis=0, keepdims=True)
    total_col = row_to_col(total)
    sub = iota((CLUSTERS, CLUSTERS), 0)
    lane = iota((CLUSTERS, CLUSTERS), 1)
    ahead = jnp.where(
        (total_col > total) | ((total_col == total) & (sub < lane)), 1.0, 0.0
    )
    order = jnp.sum(ahead, axis=0, keepdims=True)
    order_col = row_to_col(order)
    perm = order_col.astype(jnp.int32) == lane

    def owner_of(r):
        turn = lax.rem(r, 2 * planes)
        return jnp.where(turn < planes, turn, 2 * planes - 1 - turn)

    sorted_counts = dot(counts.astype(BF16), jnp.where(perm, 1.0, 0.0).astype(BF16))
    before = jnp.where((sub < lane) & (owner_of(sub) == owner_of(lane)), 1.0, 0.0)
    offset = dot(sorted_counts.astype(BF16), before.astype(BF16))
    over = jnp.where(offset + sorted_counts > cap, 1.0, 0.0)
    over = jnp.max(jnp.max(over, axis=0, keepdims=True), axis=1, keepdims=True)
    over = jnp.broadcast_to(over, (1, 128))
    flag_ref[...] = over
    flag_buf[mine] = over

    own_offset = jnp.sum(
        jnp.where(iota((planes, CLUSTERS), 0) == z, offset, 0.0), axis=0, keepdims=True
    )
    start_row = own_offset + (owner_of(iota((1, CLUSTERS), 1)) * cap).astype(F32)
    start_col = jnp.sum(jnp.where(perm, start_row, 0.0), axis=1, keepdims=True)

    def pos_step(ch, carry):
        member = iota((CLUSTERS, 128), 0) == ids_row(ch)
        base = jnp.sum(jnp.where(member, start_col, 0.0), axis=0, keepdims=True)
        pos_buf[pl.ds(ch, 1), :] = (base + rank_buf[pl.ds(ch, 1), :]).astype(jnp.int32)
        return carry

    lax.fori_loop(0, chunks, pos_step, 0)
    pos = jnp.concatenate([pos_buf[i:i + 1, :] for i in range(chunks)], axis=1)

    step = 4 if planes % 4 == 0 else 1

    def pack_step(b, ti):
        parts = []
        for j in range(step):
            dest = lax.rem(z + b * step + j, planes)
            parts.append(
                jnp.where(iota((cap, tokens), 0) + dest * cap == pos, 1.0, 0.0).astype(BF16)
            )
        packed = dot(jnp.concatenate(parts, axis=0), rows[ti]).astype(BF16)
        for j in range(step):
            dest = lax.rem(z + b * step + j, planes)
            at = pl.ds(pl.multiple_of(dest * cap, cap), cap)
            zsend[ti, at, :] = packed[j * cap:(j + 1) * cap]
            to = pl.ds(pl.multiple_of(z * cap, cap), cap)

            @pl.when(dest != z)
            def _(dest=dest, at=at, to=to):
                pltpu.make_async_remote_copy(
                    src_ref=zsend.at[ti, at, :], dst_ref=zrecv.at[ti, to, :],
                    send_sem=in_sem.at[0, ti], recv_sem=in_sem.at[1, ti],
                    device_id=ring_id(dest), device_id_type=MESH,
                ).start()

            @pl.when(dest == z)
            def _(j=j, to=to):
                zrecv[ti, to, :] = packed[j * cap:(j + 1) * cap]

        return ti

    for ti in range(4):
        own_copies[ti].wait()
        drain(rows.at[ti, pl.ds(0, (peers - 1) * per_dev), :], one_sem.at[1, ti])
        lax.fori_loop(0, planes // step, pack_step, ti)


    @pl.loop(1, peers)
    def _(j):
        pltpu.make_async_remote_copy(
            src_ref=flag_ref, dst_ref=flag_buf.at[mine],
            send_sem=flag_sem.at[0], recv_sem=flag_sem.at[1],
            device_id=plane_id(*plane_peer(j)), device_id_type=MESH,
        ).start()

    lane_l = iota((CLUSTERS, 128), 1)
    sub_l = iota((CLUSTERS, 128), 0)
    chosen = jnp.where((sub_l // planes == lane_l) & (owner_of(sub_l) == z), 1.0, 0.0).astype(BF16)
    first = dot(offset.astype(BF16), chosen).astype(jnp.int32)
    length = dot(sorted_counts.astype(BF16), chosen).astype(jnp.int32)
    slot = iota((cap, 128), 0)
    for i in range(planes):
        low = first[i:i + 1, :]
        mark = (slot >= low) & (slot < low + length[i:i + 1, :])
        marks[i * cap:(i + 1) * cap, :] = jnp.where(mark, 1.0, 0.0).astype(BF16)

    received = pl.ds(0, (planes - 1) * cap)
    scale = WIDTH ** -0.5
    blocks = slots // BLOCK_Q

    def rows_of(b):
        return pl.ds(pl.multiple_of(b * BLOCK_Q, BLOCK_Q), BLOCK_Q)

    drain(zrecv.at[0, received, :], in_sem.at[1, 0])
    drain(zrecv.at[1, received, :], in_sem.at[1, 1])

    @pl.loop(0, blocks)
    def _(b):
        at = rows_of(b)
        score = dot_nt(zrecv[0, at, :], zrecv[1]) * scale
        same = dot_nt(marks[at, :], marks[...])
        score = jnp.where(same > 0.5, score, NEG)
        top = jnp.max(score, axis=1, keepdims=True)
        expo = jnp.exp(score - top)
        prob[at, :] = (expo / jnp.sum(expo, axis=1, keepdims=True)).astype(BF16)

    drain(zrecv.at[2, received, :], in_sem.at[1, 2])
    drain(zrecv.at[0, received, :], in_sem.at[0, 0])

    @pl.loop(0, blocks)
    def _(b):
        at = rows_of(b)
        zsend[0, at, :] = dot(prob[at, :], zrecv[2]).astype(BF16)

    def give_back(ti):
        at = pl.ds(pl.multiple_of(z * cap, cap), cap)

        @pl.loop(1, planes)
        def _(d):
            dest = lax.rem(z + d, planes)
            pltpu.make_async_remote_copy(
                src_ref=zsend.at[ti, pl.ds(pl.multiple_of(dest * cap, cap), cap), :],
                dst_ref=zret.at[ti, at, :],
                send_sem=back_sem.at[0, ti], recv_sem=back_sem.at[1, ti],
                device_id=ring_id(dest), device_id_type=MESH,
            ).start()

        zret[ti, at, :] = zsend[ti, at, :]

    give_back(0)
    for ti in range(1, 4):
        drain(zrecv.at[ti, received, :], in_sem.at[0, ti])
    drain(zrecv.at[3, received, :], in_sem.at[1, 3])

    dk_acc[...] = jnp.zeros_like(dk_acc)
    dv_acc[...] = jnp.zeros_like(dv_acc)

    @pl.loop(0, blocks)
    def _(b):
        at = rows_of(b)
        grad = zrecv[3, at, :]
        part = prob[at, :]
        wide = part.astype(F32)
        dprob = dot_nt(grad, zrecv[2])
        mean = jnp.sum(wide * dprob, axis=1, keepdims=True)
        dscore = (wide * (dprob - mean) * scale).astype(BF16)
        zsend[1, at, :] = dot(dscore, zrecv[1]).astype(BF16)
        dk_acc[...] += dot_tn(dscore, zrecv[0, at, :])
        dv_acc[...] += dot_tn(part, grad)

    give_back(1)
    zsend[2] = dk_acc[...].astype(BF16)
    give_back(2)
    zsend[3] = dv_acc[...].astype(BF16)
    give_back(3)

    for ti in range(4):
        drain(rows.at[ti, pl.ds(0, (peers - 1) * per_dev), :], one_sem.at[0, ti])

    batch = 256 // per_dev if per_dev < 256 else 1
    span = batch * per_dev
    own_cols = pl.ds(pl.multiple_of((hd * lanes_y + y) * WIDTH, WIDTH), WIDTH)

    for ti in range(4):
        drain(zret.at[ti, received, :], back_sem.at[1, ti])

        @pl.loop(0, tokens // span)
        def _(b, ti=ti):
            cols = []
            for i in range(span // 128):
                row = pos_buf[pl.ds(b * (span // 128) + i, 1), :].astype(F32)
                cols.append(jnp.sum(jnp.where(eye, row, 0.0), axis=1, keepdims=True))
            place = jnp.concatenate(cols, axis=0).astype(jnp.int32)
            pick = jnp.where(iota((span, slots), 1) == place, 1.0, 0.0).astype(BF16)
            at = pl.ds(pl.multiple_of(b * span, span), span)
            rows[ti, at, :] = dot(pick, zret[ti]).astype(BF16)
            for j in range(batch):
                index = b * batch + j
                source = rows.at[ti, pl.ds(pl.multiple_of(index * per_dev, per_dev), per_dev), :]

                @pl.when(index != mine)
                def _(index=index, source=source):
                    pltpu.make_async_remote_copy(
                        src_ref=source, dst_ref=out_ref.at[ti, :, own_cols],
                        send_sem=two_sem.at[0, ti], recv_sem=two_sem.at[1, ti],
                        device_id=plane_id(index // groups, lax.rem(index, groups)),
                        device_id_type=MESH,
                    ).start()

                @pl.when(index == mine)
                def _(source=source):
                    pltpu.make_async_copy(
                        source, out_ref.at[ti, :, own_cols], own_sem.at[ti]
                    ).start()

    drain(flag_buf.at[pl.ds(0, peers - 1)], flag_sem.at[1])
    drain(flag_buf.at[pl.ds(0, peers - 1)], flag_sem.at[0])
    flags = flag_buf[0]
    for i in range(1, peers):
        flags = jnp.maximum(flags, flag_buf[i])
    flag_ref[...] = flags
    drain(ids_buf.at[pl.ds(0, lanes_y - 1)], ids_sem.at[0])
    for ti in range(4):
        drain(zrecv.at[ti, received, :], back_sem.at[0, ti])
        own = rows.at[ti, pl.ds(0, per_dev), :]
        drain(own, own_sem.at[ti])
        plane_rows = rows.at[ti, pl.ds(0, (peers - 1) * per_dev), :]
        drain(plane_rows, two_sem.at[0, ti])
        drain(plane_rows, two_sem.at[1, ti])


def attend(cap, planes, lanes_y, groups, queries, keys, values, grad_out, ids):
    per_dev = queries.shape[0]
    tokens = lanes_y * groups * per_dev
    slots = planes * cap
    dma = pltpu.SemaphoreType.DMA
    chunk_rows = tokens // 128
    return pl.pallas_call(
        functools.partial(kernel, (planes, lanes_y, groups, cap, per_dev)),
        out_shape=(
            jax.ShapeDtypeStruct((4,) + queries.shape, BF16),
            jax.ShapeDtypeStruct((1, 128), F32),
        ),
        in_specs=[pl.BlockSpec(memory_space=pl.ANY)] * 5,
        out_specs=(
            pl.BlockSpec(memory_space=pl.ANY),
            pl.BlockSpec(memory_space=pltpu.VMEM),
        ),
        scratch_shapes=[
            pltpu.VMEM(ids.shape, jnp.int32),
            pltpu.VMEM((1, CLUSTERS), F32),
            pltpu.VMEM((planes, 1, CLUSTERS), F32),
            pltpu.VMEM((lanes_y * groups, 1, 128), F32),
            pltpu.VMEM((chunk_rows, 128), F32),
            pltpu.VMEM((chunk_rows, 128), jnp.int32),
            pltpu.VMEM((4, tokens, WIDTH), BF16),
            pltpu.VMEM((4, slots, WIDTH), BF16),
            pltpu.VMEM((4, slots, WIDTH), BF16),
            pltpu.VMEM((4, slots, WIDTH), BF16),
            pltpu.VMEM((slots, slots), BF16),
            pltpu.VMEM((slots, 128), BF16),
            pltpu.VMEM((slots, WIDTH), F32),
            pltpu.VMEM((slots, WIDTH), F32),
            dma((2,)), dma((2,)), dma((2,)),
            dma((2, 4)), dma((2, 4)), dma((2, 4)), dma((2, 4)),
            dma((6,)),
        ],
        compiler_params=pltpu.CompilerParams(
            collective_id=1 if cap == TIGHT else 2,
            has_side_effects=True,
            vmem_limit_bytes=66_000_000,
        ),
        name="attend_%d" % cap,
    )(queries, keys, values, grad_out, ids)


def solution(mesh):
    seq_count, groups = mesh.shape["seq"], mesh.shape["head"]

    def body(queries, keys, values, grad_out, cluster_ids):
        lanes_y, seq_tok = cluster_ids.shape[0], cluster_ids.shape[1]
        planes = seq_count // lanes_y
        loose = lanes_y * MOST * CLUSTERS // planes
        ids = cluster_ids.reshape(lanes_y, seq_tok // 128, 128)
        arrays = (queries, keys, values, grad_out, ids)
        out, flag = attend(TIGHT, planes, lanes_y, groups, *arrays)
        out = lax.cond(
            flag[0, 0] > 0.5,
            lambda: attend(loose, planes, lanes_y, groups, *arrays)[0],
            lambda: out,
        )
        return out[0], out[1], out[2], out[3]

    row_spec = P(("seq", "head"), None)
    return jax.shard_map(
        body,
        mesh=mesh,
        in_specs=(row_spec,) * 4 + (P("head", "seq", None),),
        out_specs=(row_spec,) * 4,
        check_vma=False,
    )
```

time: 661 us -> 257 us (0.39); the launches traced: 651 us -> 254 us
  waiting for transfers between devices: 263 us -> 0 us
  Pallas kernels: 0 us -> 250 us
  local copies, waits for them, and re-layouts: 124 us -> 2.87 us
  blocking collectives: 118 us -> 0 us
  starting transfers between devices: 116 us -> 0 us
  matrix products: 28 us -> 0 us
    all_to_all x15 -> x0, waiting for transfers between devices: 263 us -> none  [the longest x1 42.8 us: body(): lax.all_to_all(q_buf, 'seq', split_axis=2, concat_axis=2, tiled=True)]
    pallas_call x0 -> x1, Pallas kernels: none -> 250 us  [attend(): pl.pallas_call(functools.partial(kernel, (planes, lanes_y, groups, cap, p...]
    all_to_all x2 -> x0, blocking collectives: 118 us -> none  [the longest x1 59.2 us: body(): lax.all_to_all(dq_own, 'seq', split_axis=2, concat_axis=2, tiled=True)]
    all_to_all x15 -> x0, starting transfers between devices: 116 us -> none  [the longest x1 19.3 us: body(): lax.all_to_all(valid, 'seq', split_axis=2, concat_axis=2, tiled=True)]
    scatter x5 -> x0, local copies, waits for them, and re-layouts: 39.9 us -> none  [the longest x4 25.3 us: pack(): jnp.zeros((total, HEAD_WIDTH), rows.dtype).at[target]]
    gather x4 -> x0, local copies, waits for them, and re-layouts: 28.5 us -> none  [unpack(): buffer.reshape(total, HEAD_WIDTH)[target]]
    all_to_all x17 -> x0, local copies, waits for them, and re-layouts: 19.5 us -> none  [the longest x2 4.03 us: body(): lax.all_to_all(unpack(dq_back), 'head', split_axis=0, concat_axis=1, tile...]
    dot_general x11 -> x0, matrix products: 19.3 us -> none  [the longest x2 4.52 us: gradients(): jnp.einsum('xyl,xla->xya', score_gradient, key_block, preferred_element_t...]
  transfers between devices with their start and end apart: 15 -> 0, of which waited for: 14 -> 0; matrix products, arithmetic and copies ran while one was open for 18% -> 0% of each run, Pallas kernels for 0% -> 0%
where the time goes in v1:
time: 257 us; the launch traced here: 254 us
  Pallas kernels  250 us (97%)
  local copies, waits for them, and re-layouts  2.87 us (1%)
    pallas_call x1, Pallas kernels, attend(): pl.pallas_call(functools.partial(kernel, (planes, lanes_y, groups, cap, p...  250 us

profile of v1, /device:TPU:1, one launch (start us, length us, event | category | flops | bytes accessed | tf_op | source)
XLA Modules:
  0.0 254.0 jit_solution(7559006974430572717)
XLA Ops:
  0.6 0.0 copy-start
  0.6 0.0 copy-start.1
  0.7 249.6 %attend_144.1 = (bf16[4,64,4096]{2,1,0:T(8,128)(2,1)}, f32[1,128]{1,0:T(1,128)}) custom-call(bf16[64,4096]{1,0:T(8,128)(2,1)} %q_ref.1, bf16[64,4096]{1,0:T(8,128)(2,1)} %k_ref.1, bf16[64,4096]{1,0:T(8,128)(2,1)} %v_ref.1, bf16[64,4096]{1,0:T(8,128)(2,1)} %g_ref.1, s32[4,4,128]{2,1,0:T(4,128)} %bitcast.11), custom_call_target="tpu_custom_call" | custom-call | tf_op jit(solution)/shard_map/attend_144/pallas_call | solution.py:402
  250.9 0.0 copy-done
  250.9 0.0 copy-done.1
  250.9 0.2 conditional.1
  251.2 2.9 %slice_bitcast_fusion.3 = (bf16[64,4096]{1,0:T(8,128)(2,1)}, bf16[64,4096]{1,0:T(8,128)(2,1)}, bf16[64,4096]{1,0:T(8,128)(2,1)}, bf16[64,4096]{1,0:T(8,128)(2,1)}) fusion(bf16[4,64,4096]{2,1,0:T(8,128)(2,1)} %get-tuple-element.44), kind=kLoop, calls=%fused_computation.3 | loop fusion | bytes 4194304 | tf_op jit(solution)/shard_map/squeeze | solution.py:456
Async XLA Ops:
  0.6 250.3 %copy-start = (bf16[64,4096]{1,0:T(8,128)(2,1)S(1)}, bf16[64,4096]{1,0:T(8,128)(2,1)}, u32[]{:S(2)}) copy-start(bf16[64,4096]{1,0:T(8,128)(2,1)} %q_ref.1) | copy-start | bytes 1572868
  0.6 250.3 %copy-start.1 = (s32[4,512,1]{1,2,0:T(1,128)S(1)}, s32[4,512,1]{1,2,0:T(1,128)}, u32[]{:S(2)}) copy-start(s32[4,512,1]{1,2,0:T(1,128)} %param.11) | copy-start | bytes 24580
